TPU v7x, 32 devices: a whole 2x2x4 slice. The times are simulated.
32 devices in a mesh: row: 8 (over y, x, core), col: 4 (over z).
Axes of the slice: x: 2, y: 2, z: 4, core: 2. Of those that a mesh axis runs over, the one named last changes fastest.
Arguments:
- fast_pos: float32 [3, 4096], P(None, ('row', 'col')), may hold values from 0 to 1
- fast_vel: float32 [3, 4096], P(None, ('row', 'col')), may hold values from -5 to 5
- fast_charge: float32 [4096], replicated, may hold values from -4 to 4
- fast_owner: int32 [4096], replicated, may hold values from 0 to 1023, as said below
- exclusions: int32 [4096, 4], replicated, may hold values from 0 to 4095, as said below
- slow_pos: float32 [3, 32, 32, 128], P(None, 'row', 'col'), may hold values from 0 to 1
- slow_vel: float32 [3, 32, 32, 128], P(None, 'row', 'col'), may hold values from -5 to 5
- slow_charge: float32 [32, 32, 128], P('row', 'col'), may hold values from -4 to 4
- neighbours: int32 [32, 32, 5], P('row', 'col'), may hold values from 0 to 24, all different within a row
Outputs:
- fast_pos_out: float32 [3, 4096], P(None, ('row', 'col'))
- fast_vel_out: float32 [3, 4096], P(None, ('row', 'col'))
- slow_pos_out: float32 [3, 32, 32, 128], P(None, 'row', 'col')
- slow_vel_out: float32 [3, 32, 32, 128], P(None, 'row', 'col')
Inputs may be any that keep to these rules, and one draw needn't show every extreme that they name: `fast_owner`: atoms a and b with a % (256) == b % (256) share an owner. `exclusions`: the partners of atom a are atoms b != a with b % (256) == a % 256; a partner may repeat. `neighbours`: the entries of one cell are distinct.
All inputs are finite; a program needn't handle non-finite values.
Results may differ from a plain program's by a relative error of at most 0.0003.
Values sent between devices are 32-bit elements; how exact they have to be, the bound alone decides.
No kernel may reach another device: no remote copies, remote signals or barrier semaphores. Data moves between devices by JAX's collectives and lax.ppermute only.
A program may use at most 64 MiB of HBM per device.

v0:
```python
import jax
import jax.numpy as jnp
from jax import lax
from jax.sharding import PartitionSpec as P

FAST = 4096
CELL = 128
INNER = 4
fast_coupling = 1.0
slow_coupling = 0.1
outer_dt = 0.2


def with_halo(x, sides, width):
    for axis, dim in sides:
        count, length = (lax.axis_size(axis), x.shape[dim])
        up = [(i, (i + 1) % count) for i in range(count)]
        down = [(j, i) for i, j in up]
        last = lax.slice_in_dim(x, length - width, length, axis=dim)
        initial = lax.slice_in_dim(x, 0, width, axis=dim)
        before = lax.ppermute(last, axis, up)
        after = lax.ppermute(initial, axis, down)
        x = jnp.concatenate([before, x, after], axis=dim)
    return x


def owner_coords(owner, total_cols):
    grid_row = (owner // total_cols).astype(jnp.float32)
    grid_col = (owner % total_cols).astype(jnp.float32)
    return jnp.stack([grid_row, grid_col, jnp.zeros_like(grid_row)])


def pair_fast(pos_a, cell_a, charge_a, exclude_a, pos_b, cell_b, charge_b, index_b):
    delta = pos_a[:, :, None] - pos_b[:, None, :] + (cell_a[:, :, None] - cell_b[:, None, :])
    dist_sq = jnp.sum(delta * delta, axis=0) + 1.0
    inverse = 1.0 / (dist_sq * jnp.sqrt(dist_sq))
    barred = jnp.any(exclude_a[:, :, None] == index_b[None, None, :], axis=1)
    weight = jnp.where(barred, jnp.float32(0.0), charge_a[:, None] * charge_b[None, :] * inverse)
    return fast_coupling * jnp.sum(weight[None] * delta, axis=2)


def slow_cells(own, views, lists):
    force = jnp.zeros((3,) + own.shape[1:], jnp.float32)
    offsets = jnp.arange(25, dtype=jnp.int32)
    for slot in range(lists.shape[-1]):
        chosen = lists[..., slot]
        pick = (chosen[..., None] == offsets).astype(jnp.float32)
        other = jnp.einsum("abo,oxabn->xabn", pick, views, precision=lax.Precision.HIGHEST)
        shift_row = (chosen // 5 - 2).astype(jnp.float32)
        shift_col = (chosen % 5 - 2).astype(jnp.float32)
        shift = jnp.stack([shift_row, shift_col, jnp.zeros_like(shift_row)])
        delta = own[0:3, :, :, :, None] - (other[0:3, :, :, None, :] + shift[:, :, :, None, None])
        dist_sq = jnp.sum(delta * delta, axis=0) + 0.5
        inverse = 1.0 / (dist_sq * jnp.sqrt(dist_sq))
        weight = other[3][:, :, None, :] * inverse
        force = force + jnp.sum(weight[None] * delta, axis=-1)
    return slow_coupling * own[3][None] * force


def fast_from_cells(frac, charge, picked):
    delta = frac[:, :, None] - picked[0:3]
    dist_sq = jnp.sum(delta * delta, axis=0) + 0.5
    inverse = 1.0 / (dist_sq * jnp.sqrt(dist_sq))
    weight = picked[3] * inverse
    return slow_coupling * charge[None, :] * jnp.sum(weight[None] * delta, axis=-1)


def per_device(
    fast_pos,
    fast_vel,
    fast_charge,
    fast_owner,
    exclusions,
    slow_pos,
    slow_vel,
    slow_charge,
    neighbours,
):
    row_count = lax.axis_size("row")
    col_count = lax.axis_size("col")
    row_index = lax.axis_index("row")
    col_index = lax.axis_index("col")
    flat_index = row_index * col_count + col_index
    piece = fast_pos.shape[1]
    cell_rows = slow_pos.shape[1]
    cell_cols = slow_pos.shape[2]
    total_cols = cell_cols * col_count
    coords = owner_coords(fast_owner, total_cols)
    block_width = col_count * piece
    block_start = row_index * block_width
    rows_cells = lax.dynamic_slice_in_dim(coords, block_start, block_width, 1)
    rows_charge = lax.dynamic_slice_in_dim(fast_charge, block_start, block_width, 0)
    rows_exclude = lax.dynamic_slice_in_dim(exclusions, block_start, block_width, 0)
    column_atoms = (
        (jnp.arange(row_count, dtype=jnp.int32) * col_count + col_index)[:, None] * piece
        + jnp.arange(piece, dtype=jnp.int32)[None, :]
    ).reshape(-1)
    column_cells = jnp.take(coords, column_atoms, axis=1)
    column_charge = jnp.take(fast_charge, column_atoms, axis=0)

    def fast_force(frac):
        rows_pos = lax.all_gather(frac, "col", axis=1, tiled=True)
        cols_pos = lax.all_gather(frac, "row", axis=1, tiled=True)
        partial_force = pair_fast(
            rows_pos,
            rows_cells,
            rows_charge,
            rows_exclude,
            cols_pos,
            column_cells,
            column_charge,
            column_atoms,
        )
        return lax.psum_scatter(partial_force, "col", scatter_dimension=1, tiled=True)

    grid_row = fast_owner // total_cols - row_index * cell_rows
    grid_col = fast_owner % total_cols - col_index * cell_cols
    inside = (grid_row >= 0) & (grid_row < cell_rows) & (grid_col >= 0) & (grid_col < cell_cols)
    local_cell = grid_row * cell_cols + grid_col
    cell_ids = jnp.arange(cell_rows * cell_cols, dtype=jnp.int32)
    select = jnp.where(
        inside[:, None] & (local_cell[:, None] == cell_ids[None, :]),
        jnp.float32(1.0),
        jnp.float32(0.0),
    )

    def slow_both(spos, frac):
        data = jnp.concatenate([spos, slow_charge[None]], axis=0)
        padded = with_halo(data, (("row", 1), ("col", 2)), 2)
        views = jnp.stack(
            [padded[:, o // 5 : o // 5 + cell_rows, o % 5 : o % 5 + cell_cols] for o in range(25)]
        )
        cell_force = slow_cells(data, views, neighbours)
        everyone = lax.all_gather(frac, ("row", "col"), axis=1, tiled=True)
        table = jnp.transpose(data, (1, 2, 0, 3)).reshape(cell_rows * cell_cols, 4 * CELL)
        picked = jnp.dot(
            select, table, precision=lax.Precision.HIGHEST, preferred_element_type=jnp.float32
        )
        picked = jnp.transpose(picked.reshape(FAST, 4, CELL), (1, 0, 2))
        partial_env = fast_from_cells(everyone, fast_charge, picked)
        summed = lax.psum(partial_env, ("row", "col"))
        own_env = lax.dynamic_slice_in_dim(summed, flat_index * piece, piece, 1)
        return (cell_force, own_env)

    half_outer = 0.5 * outer_dt
    inner_dt = outer_dt / INNER
    fast_acc = fast_force(fast_pos)
    slow_acc, env_acc = slow_both(slow_pos, fast_pos)
    slow_vel = slow_vel + half_outer * slow_acc
    fast_vel = fast_vel + half_outer * env_acc
    for inner_step in range(INNER):
        fast_vel = fast_vel + 0.5 * inner_dt * fast_acc
        fast_pos = fast_pos + inner_dt * fast_vel
        fast_acc = fast_force(fast_pos)
        fast_vel = fast_vel + 0.5 * inner_dt * fast_acc
    slow_pos = slow_pos + outer_dt * slow_vel
    slow_acc, env_acc = slow_both(slow_pos, fast_pos)
    slow_vel = slow_vel + half_outer * slow_acc
    fast_vel = fast_vel + half_outer * env_acc
    return (fast_pos, fast_vel, slow_pos, slow_vel)


def solution(mesh):
    return jax.shard_map(
        per_device,
        mesh=mesh,
        in_specs=(
            P(None, ("row", "col")),
            P(None, ("row", "col")),
            P(),
            P(),
            P(),
            P(None, "row", "col", None),
            P(None, "row", "col", None),
            P("row", "col", None),
            P("row", "col", None),
        ),
        out_specs=(
            P(None, ("row", "col")),
            P(None, ("row", "col")),
            P(None, "row", "col", None),
            P(None, "row", "col", None),
        ),
        check_vma=False,
    )
```

profile of v0, /device:TPU:0, one launch (start us, length us, event | category | flops | bytes accessed | tf_op | source)
XLA Modules:
  0.0 525.7 jit_solution(1581385438300912036)
XLA Ops:
  8.5 2.9 collective-permute-start.1
  11.6 9.6 %all_gather.38 = f32[3,1024]{1,0:T(4,128)S(1)} all-gather(f32[3,128]{1,0:T(4,128)} %param.9), channel_id=1, replica_groups=mesh['row'=8,'col'=4] {'row'}, dimensions={1}, use_global_device_ids=true | all-gather | bytes 13824 | tf_op jit(solution)/shard_map/all_gather | solution.py:103
  21.2 12.3 %all_gather.37 = f32[3,512]{1,0:T(4,128)S(1)} all-gather(f32[3,128]{1,0:T(4,128)} %param.9), channel_id=1, replica_groups=mesh['row'=8,'col'=4] {'col'}, dimensions={1}, use_global_device_ids=true | all-gather | bytes 7680 | tf_op jit(solution)/shard_map/all_gather | solution.py:102
  35.2 6.1 %gather_fusion = f32[1024]{0:T(1024)S(1)} fusion(f32[4096]{0:T(1024)S(1)} %copy-done.2, s32[1024]{0:T(1024)S(1)} %broadcast_clamp_fusion), kind=kCustom, calls=%fused_computation | custom fusion | bytes 12288 | tf_op jit(solution)/shard_map/jit(_take)/gather | solution.py:99
  41.3 2.8 gather_fusion.1
  49.0 1.5 multiply_reduce_fusion.10
  51.6 65.5 %all_gather.36 = f32[3,4096]{1,0:T(4,128)S(1)} all-gather(f32[3,128]{1,0:T(4,128)S(1)} %copy-done.7), channel_id=1, replica_groups=mesh['row'=8,'col'=4] {'row','col'}, dimensions={1}, use_global_device_ids=true | all-gather | bytes 50688 | tf_op jit(solution)/shard_map/all_gather | solution.py:134
  117.2 6.8 %convolution_bitcast_fusion.1 = f32[4,4096,128]{1,2,0:T(8,128)S(1)} fusion(s32[4096]{0:T(1024)S(1)} %get-tuple-element.54, pred[4096]{0:T(1024)(128)(4,1)S(1)} %compare_and_fusion, f32[1,4,8,128]{3,2,0,1:T(8,128)S(1)} %bitcast.458, f32[3,4,8,128]{3,2,1,0:T(8,128)S(1)} %copy-done.3), kind=kOutput, calls=%fused_computation.29 | convolution fusion | flops 805715968 | bytes 8474624 | tf_op jit(solution)/shard_map/dot_general | solution.py:136
  126.9 38.7 %psum.14 = f32[3,4096]{1,0:T(4,128)S(1)} all-reduce(f32[3,4096]{1,0:T(4,128)S(1)} %broadcast_multiply_fusion.1), channel_id=1, replica_groups=mesh['row'=8,'col'=4] {'row','col'}, use_global_device_ids=true, to_apply=%region_2.3 | all-reduce | flops 12288 | bytes 98304 | tf_op jit(solution)/shard_map/psum | solution.py:141
  166.5 9.7 %all_gather.40 = f32[3,1024]{1,0:T(4,128)S(1)} all-gather(f32[3,128]{1,0:T(4,128)S(1)} %get-tuple-element.36), channel_id=1, replica_groups=mesh['row'=8,'col'=4] {'row'}, dimensions={1}, use_global_device_ids=true | all-gather | bytes 13824 | tf_op jit(solution)/shard_map/all_gather | solution.py:103
  176.2 12.1 %all_gather.39 = f32[3,512]{1,0:T(4,128)S(1)} all-gather(f32[3,128]{1,0:T(4,128)S(1)} %get-tuple-element.36), channel_id=1, replica_groups=mesh['row'=8,'col'=4] {'col'}, dimensions={1}, use_global_device_ids=true | all-gather | bytes 7680 | tf_op jit(solution)/shard_map/all_gather | solution.py:102
  191.2 1.5 multiply_reduce_fusion.8
  193.7 17.6 %reduce-scatter.18.cloned.1.call-done = f32[128,3]{1,0:T(8,128)} async-done(((f32[512,3]{1,0:T(8,128)}), f32[128,3]{1,0:T(8,128)}) %reduce-scatter.18.cloned.1.call-update) | async-done | bytes 1552
  212.3 8.9 %all_gather.42 = f32[3,1024]{1,0:T(4,128)S(1)} all-gather(f32[3,128]{1,0:T(4,128)S(1)} %multiply_add_fusion.7), channel_id=1, replica_groups=mesh['row'=8,'col'=4] {'row'}, dimensions={1}, use_global_device_ids=true | all-gather | bytes 13824 | tf_op jit(solution)/shard_map/all_gather | solution.py:103
  221.2 11.9 %all_gather.41 = f32[3,512]{1,0:T(4,128)S(1)} all-gather(f32[3,128]{1,0:T(4,128)S(1)} %multiply_add_fusion.7), channel_id=1, replica_groups=mesh['row'=8,'col'=4] {'col'}, dimensions={1}, use_global_device_ids=true | all-gather | bytes 7680 | tf_op jit(solution)/shard_map/all_gather | solution.py:102
  234.5 1.5 fusion.73
  236.0 1.5 multiply_reduce_fusion.6
  238.5 3.8 collective-permute-start.3
  242.4 13.8 %reduce-scatter.20.cloned.1.call-done = f32[128,3]{1,0:T(8,128)} async-done(((f32[512,3]{1,0:T(8,128)}), f32[128,3]{1,0:T(8,128)}) %reduce-scatter.20.cloned.1.call-update) | async-done | bytes 1552
  257.1 8.9 %all_gather.44 = f32[3,1024]{1,0:T(4,128)S(1)} all-gather(f32[3,128]{1,0:T(4,128)S(1)} %get-tuple-element.34), channel_id=1, replica_groups=mesh['row'=8,'col'=4] {'row'}, dimensions={1}, use_global_device_ids=true | all-gather | bytes 13824 | tf_op jit(solution)/shard_map/all_gather | solution.py:103
  266.0 11.9 %all_gather.43 = f32[3,512]{1,0:T(4,128)S(1)} all-gather(f32[3,128]{1,0:T(4,128)S(1)} %get-tuple-element.34), channel_id=1, replica_groups=mesh['row'=8,'col'=4] {'col'}, dimensions={1}, use_global_device_ids=true | all-gather | bytes 7680 | tf_op jit(solution)/shard_map/all_gather | solution.py:102
  280.8 1.5 multiply_reduce_fusion.4
  283.2 17.7 %reduce-scatter.22.cloned.1.call-done = f32[128,3]{1,0:T(8,128)} async-done(((f32[512,3]{1,0:T(8,128)}), f32[128,3]{1,0:T(8,128)}) %reduce-scatter.22.cloned.1.call-update) | async-done | bytes 1552
  301.8 8.9 %all_gather.46 = f32[3,1024]{1,0:T(4,128)S(1)} all-gather(f32[3,128]{1,0:T(4,128)S(1)} %multiply_add_fusion.5), channel_id=1, replica_groups=mesh['row'=8,'col'=4] {'row'}, dimensions={1}, use_global_device_ids=true | all-gather | bytes 13824 | tf_op jit(solution)/shard_map/all_gather | solution.py:103
  310.7 12.3 %all_gather.45 = f32[3,512]{1,0:T(4,128)S(1)} all-gather(f32[3,128]{1,0:T(4,128)S(1)} %multiply_add_fusion.5), channel_id=1, replica_groups=mesh['row'=8,'col'=4] {'col'}, dimensions={1}, use_global_device_ids=true | all-gather | bytes 7680 | tf_op jit(solution)/shard_map/all_gather | solution.py:102
  325.9 1.5 multiply_reduce_fusion.2
  328.3 63.9 %all_gather.47 = f32[3,4096]{1,0:T(4,128)S(1)} all-gather(f32[3,128]{1,0:T(4,128)S(1)} %multiply_add_fusion.5), channel_id=1, replica_groups=mesh['row'=8,'col'=4] {'row','col'}, dimensions={1}, use_global_device_ids=true | all-gather | bytes 50688 | tf_op jit(solution)/shard_map/all_gather | solution.py:134
  393.7 1.8 fusion.36
  395.6 1.8 fusion.38
  397.6 1.8 fusion.32
  399.5 1.8 fusion.34
  401.5 1.8 fusion.30
  403.4 2.5 fusion.2
  407.5 7.2 %fusion.3 = (f32[3,4,8,128]{3,2,1,0:T(8,128)S(1)}, f32[4,8,128,128]{3,2,1,0:T(8,128)S(1)}, f32[4,8,128,128]{3,2,1,0:T(8,128)S(1)}, f32[4,8,128,128]{3,2,1,0:T(8,128)S(1)}, f32[3,4,8,128]{3,2,1,0:T(8,128)S(1)}) fusion(f32[4,8,128,128]{3,2,1,0:T(8,128)S(1)} %fusion.51, f32[3,4,8,128]{3,2,1,0:T(8,128)S(1)} %slice_add_fusion.8, ...), kind=kLoop, calls=%fused_computation.33 | loop fusion | flops 21995520 | bytes 10878976 | tf_op jit(solution)/shard_map/reduce_sum | solution.py:56
  417.0 8.3 %fusion.5 = (f32[3,4,8,128]{3,2,1,0:T(8,128)S(1)}, f32[3,4,8,128]{3,2,1,0:T(8,128)S(1)}, f32[3,4,8,128]{3,2,1,0:T(8,128)S(1)}) fusion(f32[4,8,128,128]{3,2,1,0:T(8,128)S(1)} %fusion.53, f32[3,4,8,128]{3,2,1,0:T(8,128)S(1)} %slice_add_fusion.7, f32[3,4,8,128]{3,2,1,0:T(8,128)S(1)} %copy-done.3, f32[3,4,8,128]{3,2,1,0:T(8,128)S(1)} %slice_add_fusion.5, ...), kind=kLoop, calls=%fused_computation.35 | loop fusion | flops 14118912 | bytes 6635520 | tf_op jit(solution)/shard_map/reduce_sum | solution.py:56
  425.4 6.8 %convolution_bitcast_fusion = f32[4,4096,128]{1,2,0:T(8,128)S(1)} fusion(s32[4096]{0:T(1024)S(1)} %get-tuple-element.54, pred[4096]{0:T(1024)(128)(4,1)S(1)} %compare_and_fusion, f32[1,4,8,128]{3,2,1,0:T(8,128)S(1)} %bitcast.464, f32[3,4,8,128]{3,2,1,0:T(8,128)S(1)} %get-tuple-element.32), kind=kOutput, calls=%fused_computation.28 | convolution fusion | flops 805715968 | bytes 8474624 | tf_op jit(solution)/shard_map/dot_general | solution.py:136
  432.2 2.6 collective-permute-start.5
  437.6 40.2 %psum.15 = f32[3,4096]{1,0:T(4,128)S(1)} all-reduce(f32[3,4096]{1,0:T(4,128)S(1)} %broadcast_multiply_fusion), channel_id=1, replica_groups=mesh['row'=8,'col'=4] {'row','col'}, use_global_device_ids=true, to_apply=%region_31.32 | all-reduce | flops 12288 | bytes 98304 | tf_op jit(solution)/shard_map/psum | solution.py:141
  478.4 4.2 collective-permute-start.7
  482.7 1.5 collective-permute-done.6
  484.7 2.3 fusion.28
  487.0 2.3 fusion.26
  489.5 2.3 fusion.22
  491.8 2.3 fusion.24
  494.0 2.3 fusion.20
  496.6 2.5 fusion.12
  500.7 7.2 %fusion.13 = (f32[3,4,8,128]{3,2,1,0:T(8,128)S(1)}, f32[4,8,128,128]{3,2,1,0:T(8,128)S(1)}, f32[4,8,128,128]{3,2,1,0:T(8,128)S(1)}, f32[4,8,128,128]{3,2,1,0:T(8,128)S(1)}, f32[3,4,8,128]{3,2,1,0:T(8,128)S(1)}) fusion(f32[4,8,128,128]{3,2,1,0:T(8,128)S(1)} %fusion.64, f32[3,4,8,128]{3,2,1,0:T(8,128)S(1)} %slice_add_fusion.3, ...), kind=kLoop, calls=%fused_computation.43 | loop fusion | flops 21995520 | bytes 10878976 | tf_op jit(solution)/shard_map/reduce_sum | solution.py:56
  510.2 8.1 %fusion.15 = (f32[3,4,8,128]{3,2,1,0:T(8,128)S(1)}, f32[3,4,8,128]{3,2,1,0:T(8,128)S(1)}, f32[3,4,8,128]{3,2,1,0:T(8,128)S(1)}) fusion(f32[4,8,128,128]{3,2,1,0:T(8,128)S(1)} %fusion.66, f32[3,4,8,128]{3,2,1,0:T(8,128)S(1)} %slice_add_fusion.2, f32[3,4,8,128]{3,2,1,0:T(8,128)S(1)} %get-tuple-element.32, f32[3,4,8,128]{3,2,1,0:T(8,128)S(1)} %slice_add_fusion, ...), kind=kLoop, calls=%fused_computation.45 | loop fusion | flops 14118912 | bytes 6635520 | tf_op jit(solution)/shard_map/reduce_sum | solution.py:56
  (204 shorter events, 43.5 us)
Async XLA Ops:
  7.2 37.4 %copy-start = (s32[4096,4]{0,1:T(4,128)S(1)}, s32[4096,4]{0,1:T(4,128)}, u32[]{:S(2)}) copy-start(s32[4096,4]{0,1:T(4,128)} %param.13) | copy-start | bytes 196612
  7.2 27.9 %copy-start.2 = (f32[4096]{0:T(1024)S(1)}, f32[4096]{0:T(1024)}, u32[]{:S(2)}) copy-start(f32[4096]{0:T(1024)} %param.11) | copy-start | bytes 49156
  7.2 158.4 %reduce-scatter.16.cloned.1.call-start = ((), (), s32[]{:S(2)}) async-start(), calls=%async_computation.5 | async-start | bytes 327680
  8.0 230.4 %collective-permute-start = (f32[4,2,8,128]{3,2,0,1:T(8,128)S(1)}, f32[4,2,8,128]{3,2,0,1:T(8,128)S(1)}, u32[]{:S(2)}, u32[]{:S(2)}) collective-permute-start(f32[4,2,8,128]{3,2,0,1:T(8,128)S(1)} %get-tuple-element.52), channel_id=1, source_target_pairs={{0,4},{4,8},{8,12},{12,16},{16,20},{20,24},{24,28},{28,0},{1,5},{5... | collective-permute-start | bytes 98312 | tf_op jit(solution)/shard_map/ppermute | solution.py:21
  8.5 229.9 %collective-permute-start.1 = (f32[4,2,8,128]{3,2,0,1:T(8,128)S(1)}, f32[4,2,8,128]{3,2,0,1:T(8,128)S(1)}, u32[]{:S(2)}, u32[]{:S(2)}) collective-permute-start(f32[4,2,8,128]{3,2,0,1:T(8,128)S(1)} %get-tuple-element.53), channel_id=1, source_target_pairs={{4,0},{8,4},{12,8},{16,12},{20,16},{24,20},{28,24},{0,28},{5,1},{9... | collective-permute-start | bytes 98312 | tf_op jit(solution)/shard_map/ppermute | solution.py:22
  49.0 2.5 copy-start.9
  49.0 2.5 copy-start.5
  49.0 2.6 copy-start.6
  49.0 2.6 copy-start.7
  49.0 68.1 %copy-start.3 = (f32[3,4,8,128]{3,2,1,0:T(8,128)S(1)}, f32[3,4,8,128]{3,2,1,0:T(8,128)}, u32[]{:S(2)}) copy-start(f32[3,4,8,128]{3,2,1,0:T(8,128)} %param.14) | copy-start | bytes 147460
  51.4 160.0 %reduce-scatter.18.cloned.1.call-start = ((), (), s32[]{:S(2)}) async-start(), calls=%async_computation.6 | async-start | bytes 327680
  125.6 40.9 %copy-start.11 = (f32[3,128]{1,0:T(4,128)S(1)}, f32[3,128]{1,0:T(4,128)}, u32[]{:S(2)}) copy-start(f32[3,128]{1,0:T(4,128)} %param.10) | copy-start | bytes 4612
  193.6 62.5 %reduce-scatter.20.cloned.1.call-start = ((), (), s32[]{:S(2)}) async-start(), calls=%async_computation.7 | async-start | bytes 327680
  238.4 62.5 %reduce-scatter.22.cloned.1.call-start = ((), (), s32[]{:S(2)}) async-start(), calls=%async_computation.8 | async-start | bytes 327680
  238.5 154.7 %collective-permute-start.2 = (f32[4,8,2,128]{3,2,0,1:T(2,128)S(1)}, f32[4,8,2,128]{3,2,0,1:T(2,128)S(1)}, u32[]{:S(2)}, u32[]{:S(2)}) collective-permute-start(f32[4,8,2,128]{3,2,0,1:T(2,128)S(1)} %get-tuple-element.45), channel_id=1, source_target_pairs={{0,1},{1,2},{2,3},{3,0},{4,5},{5,6},{6,7},{7,4},{8,9},{9,10},{10,1... | collective-permute-start | bytes 98312 | tf_op jit(solution)/shard_map/ppermute | solution.py:21
  238.5 154.6 %collective-permute-start.3 = (f32[4,8,2,128]{3,2,0,1:T(2,128)S(1)}, f32[4,8,2,128]{3,2,0,1:T(2,128)S(1)}, u32[]{:S(2)}, u32[]{:S(2)}) collective-permute-start(f32[4,8,2,128]{3,2,0,1:T(2,128)S(1)} %get-tuple-element.44), channel_id=1, source_target_pairs={{1,0},{2,1},{3,2},{0,3},{5,4},{6,5},{7,6},{4,7},{9,8},{10,9},{11,1... | collective-permute-start | bytes 98312 | tf_op jit(solution)/shard_map/ppermute | solution.py:22
  283.2 109.1 %reduce-scatter.24.cloned.1.call-start = ((), (), s32[]{:S(2)}) async-start(), calls=%async_computation.9 | async-start | bytes 327680
  301.8 26.5 %copy-start.10 = (f32[3,128]{1,0:T(4,128)}, f32[3,128]{1,0:T(4,128)S(1)}, u32[]{:S(2)}) copy-start(f32[3,128]{1,0:T(4,128)S(1)} %multiply_add_fusion.5) | copy-start | bytes 4612
  417.0 8.3 %copy-start.8 = (f32[3,4,8,128]{3,2,1,0:T(8,128)S(1)}, f32[3,4,8,128]{3,2,1,0:T(8,128)}, u32[]{:S(2)}) copy-start(f32[3,4,8,128]{3,2,1,0:T(8,128)} %param.15) | copy-start | bytes 147460
  425.3 84.9 %copy-start.4 = (f32[3,4,8,128]{3,2,1,0:T(8,128)}, f32[3,4,8,128]{3,2,1,0:T(8,128)S(1)}, u32[]{:S(2)}) copy-start(f32[3,4,8,128]{3,2,1,0:T(8,128)S(1)} %get-tuple-element.32) | copy-start | bytes 147460
  432.2 46.2 %collective-permute-start.4 = (f32[4,2,8,128]{3,2,1,0:T(8,128)S(1)}, f32[4,2,8,128]{3,2,1,0:T(8,128)S(1)}, u32[]{:S(2)}, u32[]{:S(2)}) collective-permute-start(f32[4,2,8,128]{3,2,1,0:T(8,128)S(1)} %get-tuple-element.48), channel_id=1, source_target_pairs={{0,4},{4,8},{8,12},{12,16},{16,20},{20,24},{24,28},{28,0},{1,5},{5... | collective-permute-start | bytes 98312 | tf_op jit(solution)/shard_map/ppermute | solution.py:21
  432.2 46.1 %collective-permute-start.5 = (f32[4,2,8,128]{3,2,1,0:T(8,128)S(1)}, f32[4,2,8,128]{3,2,1,0:T(8,128)S(1)}, u32[]{:S(2)}, u32[]{:S(2)}) collective-permute-start(f32[4,2,8,128]{3,2,1,0:T(8,128)S(1)} %get-tuple-element.49), channel_id=1, source_target_pairs={{4,0},{8,4},{12,8},{16,12},{20,16},{24,20},{28,24},{0,28},{5,1},{9... | collective-permute-start | bytes 98312 | tf_op jit(solution)/shard_map/ppermute | solution.py:22
  478.4 5.8 %collective-permute-start.6 = (f32[4,8,2,128]{3,2,1,0:T(2,128)S(1)}, f32[4,8,2,128]{3,2,1,0:T(2,128)S(1)}, u32[]{:S(2)}, u32[]{:S(2)}) collective-permute-start(f32[4,8,2,128]{3,2,1,0:T(2,128)S(1)} %get-tuple-element.41), channel_id=1, source_target_pairs={{0,1},{1,2},{2,3},{3,0},{4,5},{5,6},{6,7},{7,4},{8,9},{9,10},{10,1... | collective-permute-start | bytes 98312 | tf_op jit(solution)/shard_map/ppermute | solution.py:21
  478.4 5.8 %collective-permute-start.7 = (f32[4,8,2,128]{3,2,1,0:T(2,128)S(1)}, f32[4,8,2,128]{3,2,1,0:T(2,128)S(1)}, u32[]{:S(2)}, u32[]{:S(2)}) collective-permute-start(f32[4,8,2,128]{3,2,1,0:T(2,128)S(1)} %get-tuple-element.40), channel_id=1, source_target_pairs={{1,0},{2,1},{3,2},{0,3},{5,4},{6,5},{7,6},{4,7},{9,8},{10,9},{11,1... | collective-permute-start | bytes 98312 | tf_op jit(solution)/shard_map/ppermute | solution.py:22
  509.4 9.5 %copy-start.1 = (s32[4096,4]{0,1:T(4,128)S(1)}, s32[4096,4]{0,1:T(4,128)}, u32[]{:S(2)}) copy-start(s32[4096,4]{0,1:T(4,128)} %param.13) | copy-start | bytes 196612
Sparse Core Ops, SparseCore 0:
  51.5 18.8 reduce-scatter.15
  193.7 17.5 reduce-scatter.17
  238.5 17.6 reduce-scatter.19
  283.3 17.5 reduce-scatter.21
  328.4 17.6 reduce-scatter.23
where the time goes:
time: 531 us; the launch traced here: 526 us
  blocking collectives  315 us (59%)
  other arithmetic  76.8 us (14%)
  waiting for transfers between devices  50.8 us (10%)
  matrix products  34.2 us (6%)
  local copies, waits for them, and re-layouts  19.3 us (4%)
  between operations  15.2 us (3%)
  starting transfers between devices  14.4 us (3%)
    all_gather x2, blocking collectives, slow_both(): everyone = lax.all_gather(frac, ('row', 'col'), axis=1, tiled=True)  129 us
    psum x2, blocking collectives, slow_both(): summed = lax.psum(partial_env, ('row', 'col'))  78.8 us
    all_gather x5, blocking collectives, fast_force(): rows_pos = lax.all_gather(frac, 'col', axis=1, tiled=True)  60.6 us
    unnamed x10, waiting for transfers between devices  49.2 us
    all_gather x5, blocking collectives, fast_force(): cols_pos = lax.all_gather(frac, 'row', axis=1, tiled=True)  45.9 us
    reduce_sum x4, other arithmetic, slow_cells(): force = force + jnp.sum(weight[None] * delta, axis=-1)  30.7 us
    dot_general x10, matrix products, slow_cells(): jnp.einsum('abo,oxabn->xabn', pick, views, precision=lax.Precision.HIGHEST)  20.6 us
    dot_general x2, matrix products, slow_both(): jnp.dot(select, table, precision=lax.Precision.HIGHEST, preferred_element...  13.6 us
  transfers between devices with their start and end apart: 13, of which 5 were waited for; matrix products, arithmetic and copies ran while one was open for 11% of the time, Pallas kernels for 0%

commit v1 on v0

--- a/solution.py
+++ b/solution.py
@@ -138,7 +138,7 @@
         )
         picked = jnp.transpose(picked.reshape(FAST, 4, CELL), (1, 0, 2))
         partial_env = fast_from_cells(everyone, fast_charge, picked)
-        summed = lax.psum(partial_env, ("row", "col"))
+        summed = jnp.sum(lax.all_gather(partial_env, ("row", "col")), axis=0)
         own_env = lax.dynamic_slice_in_dim(summed, flat_index * piece, piece, 1)
         return (cell_force, own_env)
 

time: 531 us -> 513 us (0.966)
  blocking collectives: 315 us -> 234 us
  waiting for transfers between devices: 50.8 us -> 92.7 us
  other arithmetic: 76.8 us -> 92.3 us
    psum x2 -> x0, blocking collectives: 78.8 us -> none  [slow_both(): summed = lax.psum(partial_env, ('row', 'col'))]
    all_gather x0 -> x2, waiting for transfers between devices: none -> 34.8 us  [slow_both(): summed = jnp.sum(lax.all_gather(partial_env, ('row', 'col')), axis=0)]
    unnamed x10 -> x12, waiting for transfers between devices: 49.2 us -> 54.6 us
  transfers between devices with their start and end apart: 13 -> 15, of which waited for: 5 -> 7; matrix products, arithmetic and copies ran while one was open for 11% -> 23% of each run, Pallas kernels for 0% -> 0%
where the time goes in v1:
time: 513 us; the launch traced here: 507 us
  blocking collectives  234 us (46%)
  waiting for transfers between devices  92.7 us (18%)
  other arithmetic  92.3 us (18%)
  matrix products  36.4 us (7%)
  local copies, waits for them, and re-layouts  19.5 us (4%)
  between operations  16.7 us (3%)
  starting transfers between devices  15.1 us (3%)
    all_gather x2, blocking collectives, slow_both(): everyone = lax.all_gather(frac, ('row', 'col'), axis=1, tiled=True)  130 us
    all_gather x5, blocking collectives, fast_force(): rows_pos = lax.all_gather(frac, 'col', axis=1, tiled=True)  60.4 us
    unnamed x12, waiting for transfers between devices  54.6 us
    all_gather x5, blocking collectives, fast_force(): cols_pos = lax.all_gather(frac, 'row', axis=1, tiled=True)  44.3 us
    all_gather x2, waiting for transfers between devices, slow_both(): summed = jnp.sum(lax.all_gather(partial_env, ('row', 'col')), axis=0)  34.8 us
    reduce_sum x4, other arithmetic, slow_cells(): force = force + jnp.sum(weight[None] * delta, axis=-1)  32.1 us
    dot_general x10, matrix products, slow_cells(): jnp.einsum('abo,oxabn->xabn', pick, views, precision=lax.Precision.HIGHEST)  20.6 us
    dot_general x2, matrix products, slow_both(): jnp.dot(select, table, precision=lax.Precision.HIGHEST, preferred_element...  15.8 us
  transfers between devices with their start and end apart: 15, of which 7 were waited for; matrix products, arithmetic and copies ran while one was open for 23% of the time, Pallas kernels for 0%

profile of v1, /device:TPU:0, one launch (start us, length us, event | category | flops | bytes accessed | tf_op | source)
XLA Modules:
  0.0 507.0 jit_solution(17144930354687698313)
XLA Ops:
  9.4 2.9 collective-permute-start.1
  12.4 9.6 %all_gather.47 = f32[3,1024]{1,0:T(4,128)S(1)} all-gather(f32[3,128]{1,0:T(4,128)} %param.9), channel_id=1, replica_groups=mesh['row'=8,'col'=4] {'row'}, dimensions={1}, use_global_device_ids=true | all-gather | bytes 13824 | tf_op jit(solution)/shard_map/all_gather | solution.py:103
  22.1 12.3 %all_gather.46 = f32[3,512]{1,0:T(4,128)S(1)} all-gather(f32[3,128]{1,0:T(4,128)} %param.9), channel_id=1, replica_groups=mesh['row'=8,'col'=4] {'col'}, dimensions={1}, use_global_device_ids=true | all-gather | bytes 7680 | tf_op jit(solution)/shard_map/all_gather | solution.py:102
  36.0 6.1 %gather_fusion = f32[1024]{0:T(1024)S(1)} fusion(f32[4096]{0:T(1024)S(1)} %copy-done.2, s32[1024]{0:T(1024)S(1)} %broadcast_clamp_fusion), kind=kCustom, calls=%fused_computation | custom fusion | bytes 12288 | tf_op jit(solution)/shard_map/jit(_take)/gather | solution.py:99
  42.2 2.8 gather_fusion.1
  52.4 65.9 %all_gather.44 = f32[3,4096]{1,0:T(4,128)S(1)} all-gather(f32[3,128]{1,0:T(4,128)S(1)} %copy-done.7), channel_id=1, replica_groups=mesh['row'=8,'col'=4] {'row','col'}, dimensions={1}, use_global_device_ids=true | all-gather | bytes 50688 | tf_op jit(solution)/shard_map/all_gather | solution.py:134
  118.3 6.8 %convolution_bitcast_fusion.1 = f32[4,4096,128]{1,2,0:T(8,128)S(1)} fusion(s32[4096]{0:T(1024)S(1)} %get-tuple-element.54, pred[4096]{0:T(1024)(128)(4,1)S(1)} %compare_and_fusion, f32[1,4,8,128]{3,2,0,1:T(8,128)S(1)} %bitcast.462, f32[3,4,8,128]{3,2,1,0:T(8,128)S(1)} %copy-done.3), kind=kOutput, calls=%fused_computation.29 | convolution fusion | flops 805715968 | bytes 8474624 | tf_op jit(solution)/shard_map/dot_general | solution.py:136
  130.6 3.3 collective-permute-start.3
  133.9 1.7 collective-permute-done.2
  136.1 1.8 fusion.36
  138.0 1.8 fusion.38
  140.0 1.8 fusion.32
  141.9 1.8 fusion.34
  143.9 1.8 fusion.30
  145.8 2.5 fusion.2
  149.9 7.2 %fusion.3 = (f32[3,4,8,128]{3,2,1,0:T(8,128)S(1)}, f32[4,8,128,128]{3,2,1,0:T(8,128)S(1)}, f32[4,8,128,128]{3,2,1,0:T(8,128)S(1)}, f32[4,8,128,128]{3,2,1,0:T(8,128)S(1)}, f32[3,4,8,128]{3,2,1,0:T(8,128)S(1)}) fusion(f32[4,8,128,128]{3,2,1,0:T(8,128)S(1)} %fusion.51, f32[3,4,8,128]{3,2,1,0:T(8,128)S(1)} %slice_add_fusion.8, ...), kind=kLoop, calls=%fused_computation.33 | loop fusion | flops 21995520 | bytes 10878976 | tf_op jit(solution)/shard_map/reduce_sum | solution.py:56
  159.4 8.1 %fusion.5 = (f32[3,4,8,128]{3,2,1,0:T(8,128)S(1)}, f32[3,4,8,128]{3,2,1,0:T(8,128)S(1)}, f32[3,4,8,128]{3,2,1,0:T(8,128)S(1)}) fusion(f32[4,8,128,128]{3,2,1,0:T(8,128)S(1)} %fusion.53, f32[3,4,8,128]{3,2,1,0:T(8,128)S(1)} %slice_add_fusion.7, f32[3,4,8,128]{3,2,1,0:T(8,128)S(1)} %copy-done.3, f32[3,4,8,128]{3,2,1,0:T(8,128)S(1)} %slice_add_fusion.5, ...), kind=kLoop, calls=%fused_computation.35 | loop fusion | flops 14118912 | bytes 6635520 | tf_op jit(solution)/shard_map/reduce_sum | solution.py:56
  167.6 2.6 collective-permute-start.5
  170.2 9.0 %convolution_bitcast_fusion = f32[4,4096,128]{1,2,0:T(8,128)} fusion(s32[4096]{0:T(1024)S(1)} %get-tuple-element.54, pred[4096]{0:T(1024)(128)(4,1)S(1)} %compare_and_fusion, f32[1,4,8,128]{3,2,1,0:T(8,128)S(1)} %bitcast.468, f32[3,4,8,128]{3,2,1,0:T(8,128)S(1)} %get-tuple-element.32), kind=kOutput, calls=%fused_computation.28 | convolution fusion | flops 805715968 | bytes 8474624 | tf_op jit(solution)/shard_map/dot_general | solution.py:136
  179.3 4.6 collective-permute-start.7
  186.0 2.3 fusion.28
  188.3 2.3 fusion.26
  190.5 2.3 fusion.22
  192.9 2.3 fusion.24
  195.2 2.3 fusion.20
  197.8 2.5 fusion.12
  201.1 2.2 fusion.64
  203.2 1.9 reduce_sum.331
  205.2 8.0 %all_gather.49 = f32[3,1024]{1,0:T(4,128)S(1)} all-gather(f32[3,128]{1,0:T(4,128)S(1)} %get-tuple-element.36), channel_id=1, replica_groups=mesh['row'=8,'col'=4] {'row'}, dimensions={1}, use_global_device_ids=true | all-gather | bytes 13824 | tf_op jit(solution)/shard_map/all_gather | solution.py:103
  213.2 12.4 %all_gather.48 = f32[3,512]{1,0:T(4,128)S(1)} all-gather(f32[3,128]{1,0:T(4,128)S(1)} %get-tuple-element.36), channel_id=1, replica_groups=mesh['row'=8,'col'=4] {'col'}, dimensions={1}, use_global_device_ids=true | all-gather | bytes 7680 | tf_op jit(solution)/shard_map/all_gather | solution.py:102
  231.0 19.1 %reduce-scatter.18.cloned.1.call-done = f32[128,3]{1,0:T(8,128)} async-done(((f32[512,3]{1,0:T(8,128)}), f32[128,3]{1,0:T(8,128)}) %reduce-scatter.18.cloned.1.call-update) | async-done | bytes 1552
  251.0 8.9 %all_gather.51 = f32[3,1024]{1,0:T(4,128)S(1)} all-gather(f32[3,128]{1,0:T(4,128)S(1)} %multiply_add_fusion.7), channel_id=1, replica_groups=mesh['row'=8,'col'=4] {'row'}, dimensions={1}, use_global_device_ids=true | all-gather | bytes 13824 | tf_op jit(solution)/shard_map/all_gather | solution.py:103
  259.9 11.9 %all_gather.50 = f32[3,512]{1,0:T(4,128)S(1)} all-gather(f32[3,128]{1,0:T(4,128)S(1)} %multiply_add_fusion.7), channel_id=1, replica_groups=mesh['row'=8,'col'=4] {'col'}, dimensions={1}, use_global_device_ids=true | all-gather | bytes 7680 | tf_op jit(solution)/shard_map/all_gather | solution.py:102
  277.2 17.7 %reduce-scatter.20.cloned.1.call-done = f32[128,3]{1,0:T(8,128)} async-done(((f32[512,3]{1,0:T(8,128)}), f32[128,3]{1,0:T(8,128)}) %reduce-scatter.20.cloned.1.call-update) | async-done | bytes 1552
  295.8 8.9 %all_gather.53 = f32[3,1024]{1,0:T(4,128)S(1)} all-gather(f32[3,128]{1,0:T(4,128)S(1)} %get-tuple-element.34), channel_id=1, replica_groups=mesh['row'=8,'col'=4] {'row'}, dimensions={1}, use_global_device_ids=true | all-gather | bytes 13824 | tf_op jit(solution)/shard_map/all_gather | solution.py:103
  304.7 11.9 %all_gather.52 = f32[3,512]{1,0:T(4,128)S(1)} all-gather(f32[3,128]{1,0:T(4,128)S(1)} %get-tuple-element.34), channel_id=1, replica_groups=mesh['row'=8,'col'=4] {'col'}, dimensions={1}, use_global_device_ids=true | all-gather | bytes 7680 | tf_op jit(solution)/shard_map/all_gather | solution.py:102
  316.6 1.6 multiply_reduce_fusion.5
  322.2 17.7 %reduce-scatter.22.cloned.1.call-done = f32[128,3]{1,0:T(8,128)} async-done(((f32[512,3]{1,0:T(8,128)}), f32[128,3]{1,0:T(8,128)}) %reduce-scatter.22.cloned.1.call-update) | async-done | bytes 1552
  340.9 8.9 %all_gather.55 = f32[3,1024]{1,0:T(4,128)S(1)} all-gather(f32[3,128]{1,0:T(4,128)S(1)} %multiply_add_fusion.5), channel_id=1, replica_groups=mesh['row'=8,'col'=4] {'row'}, dimensions={1}, use_global_device_ids=true | all-gather | bytes 13824 | tf_op jit(solution)/shard_map/all_gather | solution.py:103
  349.7 11.9 %all_gather.54 = f32[3,512]{1,0:T(4,128)S(1)} all-gather(f32[3,128]{1,0:T(4,128)S(1)} %multiply_add_fusion.5), channel_id=1, replica_groups=mesh['row'=8,'col'=4] {'col'}, dimensions={1}, use_global_device_ids=true | all-gather | bytes 7680 | tf_op jit(solution)/shard_map/all_gather | solution.py:102
  361.7 63.8 %all_gather.56 = f32[3,4096]{1,0:T(4,128)S(1)} all-gather(f32[3,128]{1,0:T(4,128)S(1)} %multiply_add_fusion.5), channel_id=1, replica_groups=mesh['row'=8,'col'=4] {'row','col'}, dimensions={1}, use_global_device_ids=true | all-gather | bytes 50688 | tf_op jit(solution)/shard_map/all_gather | solution.py:134
  430.8 3.9 multiply_reduce_fusion.1
  434.7 2.4 fusion.60
  437.1 3.9 multiply_reduce_fusion
  441.7 8.7 %fusion.13 = (f32[3,4,8,128]{3,2,1,0:T(8,128)S(1)}, f32[4,8,128,128]{3,2,1,0:T(8,128)S(1)}, f32[4,8,128,128]{3,2,1,0:T(8,128)S(1)}, f32[4,8,128,128]{3,2,1,0:T(8,128)S(1)}, f32[3,4,8,128]{3,2,1,0:T(8,128)S(1)}) fusion(f32[4,8,128,128]{3,2,1,0:T(8,128)} %fusion.64, f32[3,4,8,128]{3,2,1,0:T(8,128)S(1)} %slice_add_fusion.3, ...), kind=kLoop, calls=%fused_computation.43 | loop fusion | flops 21995520 | bytes 10878976 | tf_op jit(solution)/shard_map/reduce_sum | solution.py:56
  452.7 8.1 %fusion.15 = (f32[3,4,8,128]{3,2,1,0:T(8,128)S(1)}, f32[3,4,8,128]{3,2,1,0:T(8,128)S(1)}, f32[3,4,8,128]{3,2,1,0:T(8,128)S(1)}) fusion(f32[4,8,128,128]{3,2,1,0:T(8,128)S(1)} %fusion.66, f32[3,4,8,128]{3,2,1,0:T(8,128)S(1)} %slice_add_fusion.2, f32[3,4,8,128]{3,2,1,0:T(8,128)S(1)} %get-tuple-element.32, f32[3,4,8,128]{3,2,1,0:T(8,128)S(1)} %slice_add_fusion, ...), kind=kLoop, calls=%fused_computation.45 | loop fusion | flops 14118912 | bytes 6635520 | tf_op jit(solution)/shard_map/reduce_sum | solution.py:56
  462.4 34.8 %all-gather.5.cloned.1.call-done = f32[32,3,4096]{2,1,0:T(4,128)} async-done(((f32[1,3,4096]{2,1,0:T(4,128)}), f32[32,3,4096]{2,1,0:T(4,128)}) %all-gather.5.cloned.1.call-update) | async-done | bytes 1572880 | tf_op jit(solution)/shard_map/all_gather | solution.py:141
  497.1 1.9 reduce_sum.355
  (210 shorter events, 51.3 us)
Async XLA Ops:
  8.0 37.4 %copy-start = (s32[4096,4]{0,1:T(4,128)S(1)}, s32[4096,4]{0,1:T(4,128)}, u32[]{:S(2)}) copy-start(s32[4096,4]{0,1:T(4,128)} %param.13) | copy-start | bytes 196612
  8.0 27.9 %copy-start.2 = (f32[4096]{0:T(1024)S(1)}, f32[4096]{0:T(1024)}, u32[]{:S(2)}) copy-start(f32[4096]{0:T(1024)} %param.11) | copy-start | bytes 49156
  8.0 120.8 %reduce-scatter.16.cloned.1.call-start = ((), (), s32[]{:S(2)}) async-start(), calls=%async_computation.7 | async-start | bytes 327680
  8.9 120.9 %collective-permute-start = (f32[4,2,8,128]{3,2,0,1:T(8,128)S(1)}, f32[4,2,8,128]{3,2,0,1:T(8,128)S(1)}, u32[]{:S(2)}, u32[]{:S(2)}) collective-permute-start(f32[4,2,8,128]{3,2,0,1:T(8,128)S(1)} %get-tuple-element.52), channel_id=1, source_target_pairs={{0,4},{4,8},{8,12},{12,16},{16,20},{20,24},{24,28},{28,0},{1,5},{5... | collective-permute-start | bytes 98312 | tf_op jit(solution)/shard_map/ppermute | solution.py:21
  9.4 120.4 %collective-permute-start.1 = (f32[4,2,8,128]{3,2,0,1:T(8,128)S(1)}, f32[4,2,8,128]{3,2,0,1:T(8,128)S(1)}, u32[]{:S(2)}, u32[]{:S(2)}) collective-permute-start(f32[4,2,8,128]{3,2,0,1:T(8,128)S(1)} %get-tuple-element.53), channel_id=1, source_target_pairs={{4,0},{8,4},{12,8},{16,12},{20,16},{24,20},{28,24},{0,28},{5,1},{9... | collective-permute-start | bytes 98312 | tf_op jit(solution)/shard_map/ppermute | solution.py:22
  49.8 2.5 copy-start.6
  49.8 2.5 copy-start.7
  49.8 68.4 %copy-start.3 = (f32[3,4,8,128]{3,2,1,0:T(8,128)S(1)}, f32[3,4,8,128]{3,2,1,0:T(8,128)}, u32[]{:S(2)}) copy-start(f32[3,4,8,128]{3,2,1,0:T(8,128)} %param.14) | copy-start | bytes 147460
  49.8 68.4 %copy-start.5 = (f32[4,8,128]{2,1,0:T(8,128)S(1)}, f32[4,8,128]{2,1,0:T(8,128)}, u32[]{:S(2)}) copy-start(f32[4,8,128]{2,1,0:T(8,128)} %param.16) | copy-start | bytes 49156
  52.2 151.0 %all-gather.3.cloned.1.call-start = ((), (), s32[]{:S(2)}) async-start(), calls=%async_computation.5 | async-start | bytes 2162688 | tf_op jit(solution)/shard_map/all_gather | solution.py:141
  126.7 1.8 copy-start.9
  128.4 121.7 %reduce-scatter.18.cloned.1.call-start = ((), (), s32[]{:S(2)}) async-start(), calls=%async_computation.8 | async-start | bytes 327680
  129.8 5.8 %collective-permute-start.2 = (f32[4,8,2,128]{3,2,0,1:T(2,128)S(1)}, f32[4,8,2,128]{3,2,0,1:T(2,128)S(1)}, u32[]{:S(2)}, u32[]{:S(2)}) collective-permute-start(f32[4,8,2,128]{3,2,0,1:T(2,128)S(1)} %get-tuple-element.45), channel_id=1, source_target_pairs={{0,1},{1,2},{2,3},{3,0},{4,5},{5,6},{6,7},{7,4},{8,9},{9,10},{10,1... | collective-permute-start | bytes 98312 | tf_op jit(solution)/shard_map/ppermute | solution.py:21
  130.6 5.0 collective-permute-start.3
  159.4 8.1 %copy-start.8 = (f32[3,4,8,128]{3,2,1,0:T(8,128)S(1)}, f32[3,4,8,128]{3,2,1,0:T(8,128)}, u32[]{:S(2)}) copy-start(f32[3,4,8,128]{3,2,1,0:T(8,128)} %param.15) | copy-start | bytes 147460
  167.5 285.2 %copy-start.4 = (f32[3,4,8,128]{3,2,1,0:T(8,128)}, f32[3,4,8,128]{3,2,1,0:T(8,128)S(1)}, u32[]{:S(2)}) copy-start(f32[3,4,8,128]{3,2,1,0:T(8,128)S(1)} %get-tuple-element.32) | copy-start | bytes 147460
  167.5 11.7 %collective-permute-start.4 = (f32[4,2,8,128]{3,2,1,0:T(8,128)S(1)}, f32[4,2,8,128]{3,2,1,0:T(8,128)S(1)}, u32[]{:S(2)}, u32[]{:S(2)}) collective-permute-start(f32[4,2,8,128]{3,2,1,0:T(8,128)S(1)} %get-tuple-element.48), channel_id=1, source_target_pairs={{0,4},{4,8},{8,12},{12,16},{16,20},{20,24},{24,28},{28,0},{1,5},{5... | collective-permute-start | bytes 98312 | tf_op jit(solution)/shard_map/ppermute | solution.py:21
  167.6 11.6 %collective-permute-start.5 = (f32[4,2,8,128]{3,2,1,0:T(8,128)S(1)}, f32[4,2,8,128]{3,2,1,0:T(8,128)S(1)}, u32[]{:S(2)}, u32[]{:S(2)}) collective-permute-start(f32[4,2,8,128]{3,2,1,0:T(8,128)S(1)} %get-tuple-element.49), channel_id=1, source_target_pairs={{4,0},{8,4},{12,8},{16,12},{20,16},{24,20},{28,24},{0,28},{5,1},{9... | collective-permute-start | bytes 98312 | tf_op jit(solution)/shard_map/ppermute | solution.py:22
  179.2 6.1 %collective-permute-start.6 = (f32[4,8,2,128]{3,2,1,0:T(2,128)S(1)}, f32[4,8,2,128]{3,2,1,0:T(2,128)S(1)}, u32[]{:S(2)}, u32[]{:S(2)}) collective-permute-start(f32[4,8,2,128]{3,2,1,0:T(2,128)S(1)} %get-tuple-element.41), channel_id=1, source_target_pairs={{0,1},{1,2},{2,3},{3,0},{4,5},{5,6},{6,7},{7,4},{8,9},{9,10},{10,1... | collective-permute-start | bytes 98312 | tf_op jit(solution)/shard_map/ppermute | solution.py:21
  179.3 6.2 %collective-permute-start.7 = (f32[4,8,2,128]{3,2,1,0:T(2,128)S(1)}, f32[4,8,2,128]{3,2,1,0:T(2,128)S(1)}, u32[]{:S(2)}, u32[]{:S(2)}) collective-permute-start(f32[4,8,2,128]{3,2,1,0:T(2,128)S(1)} %get-tuple-element.40), channel_id=1, source_target_pairs={{1,0},{2,1},{3,2},{0,3},{5,4},{6,5},{7,6},{4,7},{9,8},{10,9},{11,1... | collective-permute-start | bytes 98312 | tf_op jit(solution)/shard_map/ppermute | solution.py:22
  203.2 1.9 copy-start.11
  230.9 64.0 %reduce-scatter.20.cloned.1.call-start = ((), (), s32[]{:S(2)}) async-start(), calls=%async_computation.9 | async-start | bytes 327680
  277.1 62.8 %reduce-scatter.22.cloned.1.call-start = ((), (), s32[]{:S(2)}) async-start(), calls=%async_computation.10 | async-start | bytes 327680
  322.1 139.3 %reduce-scatter.24.cloned.1.call-start = ((), (), s32[]{:S(2)}) async-start(), calls=%async_computation.11 | async-start | bytes 327680
  340.8 87.5 %copy-start.10 = (f32[3,128]{1,0:T(4,128)}, f32[3,128]{1,0:T(4,128)S(1)}, u32[]{:S(2)}) copy-start(f32[3,128]{1,0:T(4,128)S(1)} %multiply_add_fusion.5) | copy-start | bytes 4612
  430.8 66.4 %all-gather.5.cloned.1.call-start = ((), (), s32[]{:S(2)}) async-start(), calls=%async_computation.6 | async-start | bytes 2162688 | tf_op jit(solution)/shard_map/all_gather | solution.py:141
  452.7 46.9 %copy-start.1 = (s32[4096,4]{0,1:T(4,128)S(1)}, s32[4096,4]{0,1:T(4,128)}, u32[]{:S(2)}) copy-start(s32[4096,4]{0,1:T(4,128)} %param.13) | copy-start | bytes 196612
Sparse Core Ops, SparseCore 0:
  52.4 18.9 reduce-scatter.15
  231.0 19.0 reduce-scatter.17
  277.2 17.5 reduce-scatter.19
  322.3 17.6 reduce-scatter.21
  430.9 18.9 reduce-scatter.23
Sparse Core Ops, SparseCore 1:
  128.5 53.1 all-gather.2
  441.7 55.4 all-gather.4
